TPU v7x, 512 devices: a whole 4x4x16 slice. The times are simulated.
512 devices in a mesh: ctx: 64 (over x, z), head: 8 (over y, core).
Axes of the slice: x: 4, y: 4, z: 16, core: 2. Of those that a mesh axis runs over, the one named last changes fastest.
Arguments:
- hidden_in: bfloat16 [65536, 2048], P('ctx', 'head'), may hold values from -6 to 6
- proj_weight: bfloat16 [2048, 3584], P(None, 'head'), may hold values from -0.125 to 0.125
- conv_weight: float32 [3, 1024], P(None, 'head'), may hold values from -3 to 3
- norm_gain: float32 [1024], P('head'), may hold values from 0.1 to 1.9
- out_weight: bfloat16 [1024, 2048], P('head'), may hold values from -0.25 to 0.25
Outputs:
- layer_out: bfloat16 [65536, 2048], P('ctx', 'head')
All inputs are finite; a program needn't handle non-finite values.
Results may differ from a plain program's by a relative error of at most 0.014.
Values may be sent and summed in bfloat16 or wider, within the bound.
A program may use at most 64 MiB of HBM per device.

v0:
```python
import jax
import jax.numpy as jnp
from jax import lax
from jax.sharding import PartitionSpec as P

DV = 64
FQK = 16
WIN = 64
CONV = 3


def shifted(value, axis, by):
    count = lax.axis_size(axis)
    pairs = [(i, i + by) for i in range(count) if 0 <= i + by < count]
    return lax.ppermute(value, axis, pairs)


def features(vector):
    vec_len = vector.shape[-1]
    square = (vector[..., :, None] * vector[..., None, :]).reshape(
        vector.shape[:-1] + (vec_len * vec_len,)
    )
    constant = jnp.ones(vector.shape[:-1] + (1,), vector.dtype)
    return jnp.concatenate(
        [constant, vector / vec_len**0.25, square / (2.0 * vec_len) ** 0.5], axis=-1
    )


def normalize(block_in):
    values = block_in.astype(jnp.float32)
    return (values * lax.rsqrt(jnp.mean(values * values, axis=-1, keepdims=True) + 1e-06)).astype(
        jnp.bfloat16
    )


def convolve(extended, conv_weight, count):
    tap_count = conv_weight.shape[0]
    total = jnp.zeros((count, extended.shape[1]), jnp.float32)
    for tap_id in range(tap_count):
        offset = tap_count - 1 - tap_id
        total = total + conv_weight[tap_id] * extended[offset : offset + count].astype(jnp.float32)
    return total.astype(jnp.bfloat16)


def per_device(hidden_in, proj_weight, conv_weight, norm_gain, out_weight):
    highest = lax.Precision.HIGHEST
    row_count = hidden_in.shape[0]
    head_count = out_weight.shape[0] // DV
    per_head = 2 * FQK + 3 * DV
    reach_rows = WIN - 1
    edge_rows = CONV - 1
    projected = jnp.dot(
        lax.all_gather(hidden_in, "head", axis=1, tiled=True),
        proj_weight,
        preferred_element_type=jnp.float32,
    ).astype(jnp.bfloat16)
    projected = projected.reshape(row_count, head_count, per_head)
    lin_query = projected[:, :, :FQK]
    lin_key = projected[:, :, FQK : 2 * FQK]
    raw_values = projected[:, :, 2 * FQK : 2 * FQK + DV].reshape(row_count, head_count * DV)
    win_query = projected[:, :, 2 * FQK + DV : 2 * FQK + 2 * DV]
    win_key = projected[:, :, 2 * FQK + 2 * DV :].reshape(row_count, head_count * DV)
    before_rows = shifted(raw_values[row_count - edge_rows :], "ctx", 1)
    conv_values = convolve(jnp.concatenate([before_rows, raw_values], 0), conv_weight, row_count)
    prev_values, prev_keys = shifted(
        (conv_values[row_count - reach_rows :], win_key[row_count - reach_rows :]), "ctx", 1
    )
    value_grid = conv_values.reshape(row_count, head_count, DV)
    value_full = value_grid.astype(jnp.float32)
    key_feat = features(lin_key.astype(jnp.float32))
    own_state = jnp.einsum("thf,thd->fhd", key_feat, value_full, precision=highest)
    feat_count = own_state.shape[0]
    flat_state = own_state.reshape(feat_count, head_count * DV)
    position = lax.axis_index("ctx")
    piece = lax.all_gather(flat_state[None], "ctx", axis=0, tiled=True)
    shard_ids = jnp.arange(piece.shape[0], dtype=jnp.int32)
    lower_mask = (shard_ids < position)[:, None, None]
    prior = jnp.sum(jnp.where(lower_mask, piece, 0.0), axis=0)
    prior_grid = prior.reshape(feat_count, head_count, DV)
    query_feat = features(lin_query.astype(jnp.float32))
    carried = jnp.einsum("thf,fhd->thd", query_feat, prior_grid, precision=highest)
    block_rows = min(row_count, 512)
    block_total = row_count // block_rows
    key_pos = jnp.arange(row_count, dtype=jnp.int32)

    def local_block(block_id):
        offset = block_id * block_rows
        query_part = lax.dynamic_slice_in_dim(lin_query, offset, block_rows, 0)
        products = jnp.einsum(
            "thf,shf->hts", query_part, lin_key, preferred_element_type=jnp.float32
        )
        scaled = products / FQK**0.5
        query_pos = offset + jnp.arange(block_rows, dtype=jnp.int32)
        visible = key_pos[None, :] <= query_pos[:, None]
        kernel = jnp.where(visible[None], 1.0 + scaled + 0.5 * scaled * scaled, 0.0).astype(
            jnp.bfloat16
        )
        return jnp.einsum("hts,shd->thd", kernel, value_grid, preferred_element_type=jnp.float32)

    own_part = lax.map(local_block, jnp.arange(block_total, dtype=jnp.int32)).reshape(
        row_count, head_count, DV
    )
    lin = carried + own_part
    ext_keys = normalize(
        jnp.concatenate([prev_keys, win_key], 0).reshape(row_count + reach_rows, head_count, DV)
    )
    ext_values = jnp.concatenate([prev_values, conv_values], 0).reshape(
        row_count + reach_rows, head_count, DV
    )
    query_norm = normalize(win_query)
    first_token = position * row_count
    shift_ids = (
        jnp.arange(block_rows + reach_rows, dtype=jnp.int32)[None, :]
        - jnp.arange(block_rows, dtype=jnp.int32)[:, None]
    )
    band = (shift_ids >= 0) & (shift_ids <= reach_rows)

    def window_block(block_id):
        offset = block_id * block_rows
        query_part = lax.dynamic_slice_in_dim(query_norm, offset, block_rows, 0)
        key_part = lax.dynamic_slice_in_dim(ext_keys, offset, block_rows + reach_rows, 0)
        value_part = lax.dynamic_slice_in_dim(ext_values, offset, block_rows + reach_rows, 0)
        scores = (
            jnp.einsum("thd,shd->hts", query_part, key_part, preferred_element_type=jnp.float32)
            / DV**0.5
        )
        global_pos = (
            first_token + offset + jnp.arange(block_rows + reach_rows, dtype=jnp.int32) - reach_rows
        )
        allowed = band & (global_pos >= 0)[None, :]
        expo = jnp.where(allowed[None], jnp.exp(scores), 0.0)
        weights = (expo / jnp.sum(expo, axis=-1, keepdims=True)).astype(jnp.bfloat16)
        return jnp.einsum("hts,shd->thd", weights, value_part, preferred_element_type=jnp.float32)

    window = lax.map(window_block, jnp.arange(block_total, dtype=jnp.int32)).reshape(
        row_count, head_count, DV
    )
    mean_sq = jnp.mean(lin * lin, axis=-1, keepdims=True)
    gain_grid = norm_gain.reshape(head_count, DV)
    mixed_heads = (lin * lax.rsqrt(mean_sq + 1e-05) * gain_grid + window).astype(jnp.bfloat16)
    mixed_flat = mixed_heads.reshape(row_count, head_count * DV)
    partial_out = jnp.dot(mixed_flat, out_weight, preferred_element_type=jnp.float32)
    return lax.psum_scatter(
        partial_out.astype(jnp.bfloat16), "head", scatter_dimension=1, tiled=True
    )


def solution(mesh):
    return jax.shard_map(
        per_device,
        mesh=mesh,
        in_specs=(P("ctx", "head"), P(None, "head"), P(None, "head"), P("head"), P("head", None)),
        out_specs=P("ctx", "head"),
        check_vma=False,
    )
```

profile of v0, /device:TPU:4, one launch (start us, length us, event | category | flops | bytes accessed | tf_op | source)
XLA Modules:
  0.0 292.0 jit_solution(8523061620894326594)
XLA Ops:
  7.3 0.8 slice_bitcast_fusion.2
  8.1 49.0 %all-gather.3.cloned.1.call-done = bf16[1024,2048]{1,0:T(8,128)(2,1)} async-done(((bf16[1024,256]{1,0:T(8,128)(2,1)}), bf16[1024,2048]{1,0:T(8,128)(2,1)}) %all-gather.3.cloned.1.call-update) | async-done | bytes 4194320 | tf_op jit(solution)/shard_map/all_gather | solution.py:53
  57.1 4.3 %convolution_convert_fusion.1 = bf16[1024,448]{0,1:T(8,128)(2,1)S(1)} fusion(bf16[1024,2048]{1,0:T(8,128)(2,1)} %all-gather.3.cloned.1.call-done, bf16[2048,448]{0,1:T(8,128)(2,1)S(1)} %copy-done), kind=kOutput, calls=%fused_computation.46 | convolution fusion | flops 1879506944 | bytes 6946816 | tf_op jit(solution)/shard_map/dot_general | solution.py:52
  62.2 3.5 %collective-permute-start = (bf16[2,128]{0,1:T(8,128)(2,1)S(1)}, bf16[2,128]{0,1:T(8,128)(2,1)S(1)}, u32[]{:S(2)}, u32[]{:S(2)}) collective-permute-start(bf16[2,128]{0,1:T(8,128)(2,1)S(1)} %bitcast.73), channel_id=1, source_target_pairs={{0,8},{8,16},{16,24},{24,32},{32,40},{40,48},{48,56},{56,64},{64,7... | collective-permute-start | bytes 1544 | tf_op jit(solution)/shard_map/ppermute | solution.py:15
  66.0 4.1 %collective-permute-done = bf16[2,128]{0,1:T(8,128)(2,1)S(1)} collective-permute-done((bf16[2,128]{0,1:T(8,128)(2,1)S(1)}, bf16[2,128]{0,1:T(8,128)(2,1)S(1)}, u32[]{:S(2)}, u32[]{:S(2)}) %collective-permute-start) | collective-permute-done | bytes 544 | tf_op jit(solution)/shard_map/ppermute | solution.py:15
  70.1 1.1 add_convert_fusion.1
  71.2 2.5 fusion.29
  75.3 1.9 collective-permute-start.2
  78.1 1.6 multiply_multiply_fusion
  79.7 1.4 slice.68
  81.2 3.1 %collective-permute-start.1 = (bf16[63,128]{0,1:T(8,128)(2,1)}, bf16[63,128]{0,1:T(8,128)(2,1)}, u32[]{:S(2)}, u32[]{:S(2)}) collective-permute-start(bf16[63,128]{0,1:T(8,128)(2,1)} %slice.68), channel_id=1, source_target_pairs={{0,8},{8,16},{16,24},{24,32},{32,40},{40,48},{48,56},{56,64},{64,7... | collective-permute-start | bytes 48392 | tf_op jit(solution)/shard_map/ppermute | solution.py:15
  84.4 14.3 %while.26 = (s32[]{:T(128)}, f32[2,512,2,64]{1,0,3,2:T(2,128)S(1)}, s32[2]{0:T(128)S(1)}, bf16[1024,2,16]{0,2,1:T(8,128)(2,1)}, bf16[1024,2,16]{0,2,1:T(8,128)(2...) while((s32[]{:T(128)}, f32[2,512,2,64]{1,0,3,2:T(2,128)S(1)}, ...), condition=%wide.region_2.3_spmd.clone, body=%wide.region_1.2_spmd.clone.sunk | while | flops 175636992 | bytes 2724019 | solution.py:100
  86.0 2.7 fusion.74
  89.1 2.4 dynamic_update_slice.17
  93.2 2.7 fusion.74
  96.2 2.4 dynamic_update_slice.17
  98.7 1.2 reshape.143
  99.9 0.9 fusion.47
  100.9 0.9 fusion.48
  101.8 1.1 pad_maximum_fusion
  103.0 14.0 %while.27 = (s32[]{:T(128)}, f32[2,512,2,64]{1,0,3,2:T(2,128)S(1)}, s32[2]{0:T(128)S(1)}, bf16[1087,2,64]{0,2,1:T(8,128)(2,1)S(1)}, s32[]{:T(128)}, /*index=5*/b...) while((s32[]{:T(128)}, f32[2,512,2,64]{1,0,3,2:T(2,128)S(1)}, ...), condition=%wide.region_8.9_spmd.clone, body=%wide.region_6.8_spmd.clone.sunk | while | flops 156327104 | bytes 7377774 | solution.py:135
  104.6 1.9 fusion.77
  106.5 0.8 fusion.78
  107.6 2.4 dynamic_update_slice.18
  111.6 1.9 fusion.77
  113.5 0.8 fusion.78
  114.6 2.4 dynamic_update_slice.18
  117.5 114.2 %all-gather.5.cloned.1.call-done = f32[64,273,128]{2,1,0:T(8,128)} async-done(((f32[1,273,128]{2,1,0:T(8,128)}), f32[64,273,128]{2,1,0:T(8,128)}) %all-gather.5.cloned.1.call-update) | async-done | bytes 8945680 | tf_op jit(solution)/shard_map/all_gather | solution.py:75
  231.8 4.7 %select_reduce_fusion = f32[273,128]{1,0:T(8,128)S(1)} fusion(f32[64,273,128]{2,1,0:T(8,128)} %all-gather.5.cloned.1.call-done, pred[64]{0:T(512)(128)(4,1)S(1)} %iota_compare_fusion.1), kind=kLoop, calls=%fused_computation.32 | loop fusion | flops 4437888 | bytes 9085504 | tf_op jit(solution)/shard_map/reduce_sum | solution.py:78
  236.6 3.7 %multiply_reduce_fusion = (f32[1024,2]{0,1:T(2,128)S(1)}, f32[1024,2,64]{0,2,1:T(8,128)S(1)}) fusion(f32[1024,2,64]{0,2,1:T(8,128)S(1)} %copy-done.1, f32[273,2,64]{0,2,1:T(8,128)S(1)} %bitcast.70, f32[1024,2,256]{0,2,1:T(8,128)} %bitcast.59, f32[1024,2,16]{0,2,1:T(8,128)S(1)} %get-tuple-element.255, f32[273]{0:T(512)S(1)} %pad.7.clone), kind=kOutput, calls=%fused_computation.60 | convolution fusion | flops 430901248 | bytes 3425860 | tf_op jit(solution)/shard_map/thf,fhd->thd/dot_general | solution.py:81
  240.5 3.2 %convolution_convert_fusion = bf16[1024,2048]{1,0:T(8,128)(2,1)} fusion(bf16[1024,128]{0,1:T(8,128)(2,1)S(1)} %bitcast.68, bf16[128,2048]{1,0:T(8,128)(2,1)S(1)} %copy-done.2), kind=kOutput, calls=%fused_computation.33 | convolution fusion | flops 538968064 | bytes 4980736 | tf_op jit(solution)/shard_map/dot_general | solution.py:142
  243.7 41.7 %reduce-scatter.2.cloned.1.call-done = bf16[1024,256]{1,0:T(8,128)(2,1)} async-done(((bf16[1024,2048]{1,0:T(8,128)(2,1)}), bf16[1024,256]{1,0:T(8,128)(2,1)}) %reduce-scatter.2.cloned.1.call-update) | async-done | bytes 524304 | tf_op jit(solution)/shard_map/reduce_scatter | solution.py:143
  (54 shorter events, 10.1 us)
Async XLA Ops:
  6.5 50.6 %copy-start = (bf16[2048,448]{0,1:T(8,128)(2,1)S(1)}, bf16[2048,448]{0,1:T(8,128)(2,1)}, u32[]{:S(2)}) copy-start(bf16[2048,448]{0,1:T(8,128)(2,1)} %param.10) | copy-start | bytes 5505028
  6.5 50.6 %all-gather.3.cloned.1.call-start = ((), (), s32[]{:S(2)}) async-start(), calls=%async_computation.1 | async-start | bytes 4718592 | tf_op jit(solution)/shard_map/all_gather | solution.py:53
  7.3 224.5 %all-gather.5.cloned.1.call-start = ((), (), s32[]{:S(2)}) async-start(), calls=%async_computation.2 | async-start | bytes 9318400 | tf_op jit(solution)/shard_map/all_gather | solution.py:75
  62.2 7.9 %collective-permute-start = (bf16[2,128]{0,1:T(8,128)(2,1)S(1)}, bf16[2,128]{0,1:T(8,128)(2,1)S(1)}, u32[]{:S(2)}, u32[]{:S(2)}) collective-permute-start(bf16[2,128]{0,1:T(8,128)(2,1)S(1)} %bitcast.73), channel_id=1, source_target_pairs={{0,8},{8,16},{16,24},{24,32},{32,40},{40,48},{48,56},{56,64},{64,7... | collective-permute-start | bytes 1544 | tf_op jit(solution)/shard_map/ppermute | solution.py:15
  65.9 8.6 %copy-start.3 = (f32[128]{0:T(128)S(1)}, f32[128]{0:T(128)}, u32[]{:S(2)}) copy-start(f32[128]{0:T(128)} %param.12) | copy-start | bytes 1540
  74.5 211.0 %reduce-scatter.2.cloned.1.call-start = ((), (), s32[]{:S(2)}) async-start(), calls=%async_computation.3 | async-start | bytes 4718592 | tf_op jit(solution)/shard_map/reduce_scatter | solution.py:143
  75.3 24.6 %collective-permute-start.2 = (bf16[63,128]{0,1:T(8,128)(2,1)}, bf16[63,128]{0,1:T(8,128)(2,1)}, u32[]{:S(2)}, u32[]{:S(2)}) collective-permute-start(bf16[63,128]{0,1:T(8,128)(2,1)} %bitcast.14), channel_id=1, source_target_pairs={{0,8},{8,16},{16,24},{24,32},{32,40},{40,48},{48,56},{56,64},{64,7... | collective-permute-start | bytes 48392 | tf_op jit(solution)/shard_map/ppermute | solution.py:15
  81.2 20.6 %collective-permute-start.1 = (bf16[63,128]{0,1:T(8,128)(2,1)}, bf16[63,128]{0,1:T(8,128)(2,1)}, u32[]{:S(2)}, u32[]{:S(2)}) collective-permute-start(bf16[63,128]{0,1:T(8,128)(2,1)} %slice.68), channel_id=1, source_target_pairs={{0,8},{8,16},{16,24},{24,32},{32,40},{40,48},{48,56},{56,64},{64,7... | collective-permute-start | bytes 48392 | tf_op jit(solution)/shard_map/ppermute | solution.py:15
  117.5 119.1 %copy-start.1 = (f32[1024,2,64]{0,2,1:T(8,128)S(1)}, f32[1024,2,64]{0,2,1:T(8,128)}, u32[]{:S(2)}) copy-start(f32[1024,2,64]{0,2,1:T(8,128)} %reshape.143) | copy-start | bytes 1572868
  236.6 3.9 %copy-start.2 = (bf16[128,2048]{1,0:T(8,128)(2,1)S(1)}, bf16[128,2048]{1,0:T(8,128)(2,1)}, u32[]{:S(2)}) copy-start(bf16[128,2048]{1,0:T(8,128)(2,1)} %param.13) | copy-start | bytes 1572868
Sparse Core Ops, SparseCore 0:
  9.4 47.6 all-gather.2
  74.6 157.0 all-gather.4
  243.9 41.5 reduce-scatter.1
where the time goes:
time: 293 us; the launch traced here: 292 us
  waiting for transfers between devices  210 us (72%)
  matrix products  24.6 us (8%)
  local copies, waits for them, and re-layouts  19.4 us (7%)
  other arithmetic  13.4 us (5%)
  between operations  13.3 us (5%)
  starting transfers between devices  8.51 us (3%)
    all_gather x1, waiting for transfers between devices, per_device(): piece = lax.all_gather(flat_state[None], 'ctx', axis=0, tiled=True)  114 us
    all_gather x1, waiting for transfers between devices, per_device(): lax.all_gather(hidden_in, 'head', axis=1, tiled=True)  49 us
    reduce_scatter x1, waiting for transfers between devices, per_device(): lax.psum_scatter(partial_out.astype(jnp.bfloat16), 'head', scatter_dimens...  41.7 us
    dynamic_update_slice x8, local copies, waits for them, and re-layouts, per_device(): lax.map(local_block, jnp.arange(block_total, dtype=jnp.int32))  10.9 us
    ppermute x3, starting transfers between devices, shifted(): return lax.ppermute(value, axis, pairs)  8.42 us
  transfers between devices with their start and end apart: 6, of which 4 were waited for; matrix products, arithmetic and copies ran while one was open for 12% of the time, Pallas kernels for 0%

commit v1 on v0

--- a/solution.py
+++ b/solution.py
@@ -72,7 +72,14 @@
     feat_count = own_state.shape[0]
     flat_state = own_state.reshape(feat_count, head_count * DV)
     position = lax.axis_index("ctx")
-    piece = lax.all_gather(flat_state[None], "ctx", axis=0, tiled=True)
+
+    def settle_slots_over_axis(x0, shard_axis):
+        local_part = lax.all_to_all(
+            jnp.stack([x0 for _ in range(lax.psum(1, shard_axis))], 0), shard_axis, 0, 0
+        )
+        return jnp.concatenate(local_part, 0)
+
+    piece = settle_slots_over_axis(flat_state[None], "ctx")
     shard_ids = jnp.arange(piece.shape[0], dtype=jnp.int32)
     lower_mask = (shard_ids < position)[:, None, None]
     prior = jnp.sum(jnp.where(lower_mask, piece, 0.0), axis=0)

time: 293 us -> 564 us (1.92)
  the two profiles are of different devices: /device:TPU:4 before, /device:TPU:2 now
where the time goes in v1:
time: 564 us
  waiting for transfers between devices  457 us (81%)
  local copies, waits for them, and re-layouts  25.5 us (5%)
  starting transfers between devices  25.5 us (5%)
  matrix products  25.3 us (4%)
  other arithmetic  14.1 us (2%)
  between operations  13.7 us (2%)
    ppermute x3, waiting for transfers between devices, shifted(): return lax.ppermute(value, axis, pairs)  361 us
    all_gather x1, waiting for transfers between devices, per_device(): lax.all_gather(hidden_in, 'head', axis=1, tiled=True)  49.1 us
    reduce_scatter x1, waiting for transfers between devices, per_device(): lax.psum_scatter(partial_out.astype(jnp.bfloat16), 'head', scatter_dimens...  46.2 us
    all_to_all x1, starting transfers between devices, settle_slots_over_axis(): lax.all_to_all(jnp.stack([x0 for _ in range(lax.psum(1, shard_axis))], 0)...  15.1 us
  transfers between devices with their start and end apart: 6, of which 4 were waited for; matrix products, arithmetic and copies ran while one was open for 6% of the time, Pallas kernels for 0%

profile of v1, /device:TPU:2, one launch (start us, length us, event | category | flops | bytes accessed | tf_op | source)
XLA Modules:
  0.0 563.8 jit_solution(12853094850958260970)
XLA Ops:
  8.1 49.1 %all-gather.2.cloned.1.call-done = bf16[1024,2048]{1,0:T(8,128)(2,1)} async-done(((bf16[1024,256]{1,0:T(8,128)(2,1)}), bf16[1024,2048]{1,0:T(8,128)(2,1)}) %all-gather.2.cloned.1.call-update) | async-done | bytes 4194320 | tf_op jit(solution)/shard_map/all_gather | solution.py:53
  57.1 4.3 convolution_convert_fusion.1
  62.2 3.5 collective-permute-start
  66.0 4.1 collective-permute-done
  70.1 1.0 add_convert_fusion.1
  71.2 3.2 fusion.30
  74.4 1.0 copy.21
  75.4 5.9 %stack.3 = f32[64,1,273,128]{3,1,2,0:T(1,128)} broadcast(f32[273,128]{1,0:T(8,128)S(1)} %copy.21), dimensions={2,3} | broadcast | bytes 9085440 | tf_op jit(solution)/shard_map/stack | solution.py:78
  81.3 15.1 %all-to-all-start = ((f32[64,1,273,128]{3,1,2,0:T(1,128)}), f32[64,1,273,128]{3,1,2,0:T(1,128)}, u32[]{:S(2)}, u32[]{:S(2)}) async-start(f32[64,1,273,128]{3,1,2,0:T(1,128)} %stack.3), calls=%async_computation | async-start | bytes 17891328 | tf_op jit(solution)/shard_map/all_to_all | solution.py:77
  97.3 3.4 collective-permute-start.2
  101.5 1.6 multiply_multiply_fusion
  103.1 1.4 slice.68
  104.5 3.5 collective-permute-start.1
  108.2 14.3 %while.26 = (s32[]{:T(128)}, f32[2,512,2,64]{1,0,3,2:T(2,128)S(1)}, s32[2]{0:T(128)S(1)}, bf16[1024,2,16]{0,2,1:T(8,128)(2,1)}, bf16[1024,2,16]{0,2,1:T(8,128)(2...) while((s32[]{:T(128)}, f32[2,512,2,64]{1,0,3,2:T(2,128)S(1)}, ...), condition=%wide.region_2.3_spmd.clone, body=%wide.region_1.2_spmd.clone.sunk | while | flops 175636992 | bytes 2724019 | solution.py:107
  109.9 2.7 fusion.75
  112.9 2.4 dynamic_update_slice.17
  117.0 2.7 fusion.75
  120.1 2.4 dynamic_update_slice.17
  122.5 1.2 reshape.151
  123.8 356.9 %collective-permute-done.2 = bf16[63,128]{0,1:T(8,128)(2,1)} collective-permute-done((bf16[63,128]{0,1:T(8,128)(2,1)}, bf16[63,128]{0,1:T(8,128)(2,1)}, u32[]{:S(2)}, u32[]{:S(2)}) %collective-permute-start.2) | collective-permute-done | bytes 16160 | tf_op jit(solution)/shard_map/ppermute | solution.py:15
  480.7 0.9 fusion.48
  481.6 0.9 fusion.49
  482.6 1.1 pad_maximum_fusion
  483.8 13.8 %while.27 = (s32[]{:T(128)}, f32[2,512,2,64]{1,0,3,2:T(2,128)S(1)}, s32[2]{0:T(128)S(1)}, bf16[1087,2,64]{0,2,1:T(8,128)(2,1)S(1)}, s32[]{:T(128)}, /*index=5*/b...) while((s32[]{:T(128)}, f32[2,512,2,64]{1,0,3,2:T(2,128)S(1)}, ...), condition=%wide.region_8.9_spmd.clone, body=%wide.region_6.8_spmd.clone.sunk | while | flops 156327104 | bytes 7377774 | solution.py:142
  485.3 1.9 fusion.78
  488.3 2.4 dynamic_update_slice.18
  492.2 1.9 fusion.78
  495.2 2.4 dynamic_update_slice.18
  498.1 5.4 fusion.29
  503.6 3.7 multiply_reduce_fusion
  507.5 3.2 convolution_convert_fusion
  510.8 46.2 %reduce-scatter.2.cloned.1.call-done = bf16[1024,256]{1,0:T(8,128)(2,1)} async-done(((bf16[1024,2048]{1,0:T(8,128)(2,1)}), bf16[1024,256]{1,0:T(8,128)(2,1)}) %reduce-scatter.2.cloned.1.call-update) | async-done | bytes 524304 | tf_op jit(solution)/shard_map/reduce_scatter | solution.py:150
  (54 shorter events, 11.6 us)
Async XLA Ops:
  6.5 50.6 %copy-start = (bf16[2048,448]{0,1:T(8,128)(2,1)S(1)}, bf16[2048,448]{0,1:T(8,128)(2,1)}, u32[]{:S(2)}) copy-start(bf16[2048,448]{0,1:T(8,128)(2,1)} %param.10) | copy-start | bytes 5505028
  6.5 50.6 %all-gather.2.cloned.1.call-start = ((), (), s32[]{:S(2)}) async-start(), calls=%async_computation.2 | async-start | bytes 4718592 | tf_op jit(solution)/shard_map/all_gather | solution.py:53
  62.2 7.9 %collective-permute-start = (bf16[2,128]{0,1:T(8,128)(2,1)S(1)}, bf16[2,128]{0,1:T(8,128)(2,1)S(1)}, u32[]{:S(2)}, u32[]{:S(2)}) collective-permute-start(bf16[2,128]{0,1:T(8,128)(2,1)S(1)} %bitcast.77), channel_id=1, source_target_pairs={{0,8},{8,16},{16,24},{24,32},{32,40},{40,48},{48,56},{56,64},{64,7... | collective-permute-start | bytes 1544 | tf_op jit(solution)/shard_map/ppermute | solution.py:15
  81.3 15.2 %copy-start.3 = (f32[128]{0:T(128)S(1)}, f32[128]{0:T(128)}, u32[]{:S(2)}) copy-start(f32[128]{0:T(128)} %param.12) | copy-start | bytes 1540
  81.3 416.8 %all-to-all-start = ((f32[64,1,273,128]{3,1,2,0:T(1,128)}), f32[64,1,273,128]{3,1,2,0:T(1,128)}, u32[]{:S(2)}, u32[]{:S(2)}) async-start(f32[64,1,273,128]{3,1,2,0:T(1,128)} %stack.3), calls=%async_computation | async-start | bytes 17891328 | tf_op jit(solution)/shard_map/all_to_all | solution.py:77
  96.4 460.5 %reduce-scatter.2.cloned.1.call-start = ((), (), s32[]{:S(2)}) async-start(), calls=%async_computation.3 | async-start | bytes 4718592 | tf_op jit(solution)/shard_map/reduce_scatter | solution.py:150
  97.3 383.4 %collective-permute-start.2 = (bf16[63,128]{0,1:T(8,128)(2,1)}, bf16[63,128]{0,1:T(8,128)(2,1)}, u32[]{:S(2)}, u32[]{:S(2)}) collective-permute-start(bf16[63,128]{0,1:T(8,128)(2,1)} %bitcast.15), channel_id=1, source_target_pairs={{0,8},{8,16},{16,24},{24,32},{32,40},{40,48},{48,56},{56,64},{64,7... | collective-permute-start | bytes 48392 | tf_op jit(solution)/shard_map/ppermute | solution.py:15
  104.5 378.0 %collective-permute-start.1 = (bf16[63,128]{0,1:T(8,128)(2,1)}, bf16[63,128]{0,1:T(8,128)(2,1)}, u32[]{:S(2)}, u32[]{:S(2)}) collective-permute-start(bf16[63,128]{0,1:T(8,128)(2,1)} %slice.68), channel_id=1, source_target_pairs={{0,8},{8,16},{16,24},{24,32},{32,40},{40,48},{48,56},{56,64},{64,7... | collective-permute-start | bytes 48392 | tf_op jit(solution)/shard_map/ppermute | solution.py:15
  498.1 5.5 copy-start.1
  503.6 3.9 copy-start.2
Sparse Core Ops, SparseCore 0:
  9.4 47.6 all-gather.1
  510.9 45.9 reduce-scatter.1
